TPU v7x, 32 devices: a whole 2x2x4 slice. The times are simulated.
32 devices in a mesh: seq: 2 (over y), dom: 8 (over z, x), tm: 2 (over core).
Axes of the slice: x: 2, y: 2, z: 4, core: 2. Of those that a mesh axis runs over, the one named last changes fastest.
Arguments:
- particles: bfloat16 [4, 1536, 128], P('tm', ('seq', 'dom')), parts along dimension 1, may hold values from -6 to 6
- log_weight: float32 [4, 1536], P('tm', ('seq', 'dom')), parts along dimension 1, may hold values from -13 to 313
- trans_weight: bfloat16 [128, 128], replicated, may hold values from -0.5 to 0.5
- precision: float32 [128], replicated, may hold values from 0.2 to 2
Outputs:
- smoothed: float32 [4, 1536], P('tm', ('seq', 'dom')), parts along dimension 1
- score: float32 [256, 128], P('seq'), parts along dimension 0
There are 2 independent parts, one for each index of `seq`. A program takes and returns all parts, laid end to end along the dimension named above; an argument that names none is the same for every part. Nothing has to cross between parts.
All inputs are finite; a program needn't handle non-finite values.
Results may differ from a plain program's by a relative error of at most 0.0061.
Values may be sent and summed in bfloat16 or wider, within the bound.
A program may use at most 64 MiB of HBM per device.

v0:
```python
import jax
import jax.numpy as jnp
from jax import lax
from jax.sharding import PartitionSpec as P

exact_mode = lax.Precision.HIGHEST


def from_behind(x, axis, by):
    size = lax.axis_size(axis)
    pairs = [(i, i + by) for i in range(size) if 0 <= i + by < size]
    return lax.ppermute(x, axis, pairs)


def block_size(length):
    best = 1
    for trial in range(1, min(length, 512) + 1):
        if length % trial == 0:
            best = trial
    return best


def project_rows(rows, precision, weight_full):
    return jnp.dot(rows.astype(jnp.float32) * precision, weight_full, precision=exact_mode).astype(
        jnp.bfloat16
    )


def pair_scores(row_proj, column_rows, column_bias):
    return (
        jnp.einsum("id,jd->ij", row_proj, column_rows, preferred_element_type=jnp.float32)
        + column_bias[None, :]
    )


def make_norm_fold(row_proj, bias_row, carried, block_in, first_row):
    length = block_in.shape[0]
    size = block_size(length)

    def inner(position, state):
        row_top, row_total = state
        offset = position * size
        column_rows = lax.dynamic_slice_in_dim(block_in, offset, size, 0)
        bias_part = lax.dynamic_slice_in_dim(bias_row, first_row + offset, size, 0)
        scores = pair_scores(row_proj, column_rows, bias_part)
        new_top = jnp.maximum(row_top, jnp.max(scores, axis=1))
        row_total = row_total * jnp.exp(row_top - new_top) + jnp.sum(
            jnp.exp(scores - new_top[:, None]), axis=1
        )
        return (new_top, row_total)

    return lax.fori_loop(0, length // size, inner, carried)


def make_column_fold(row_proj, bias_row, row_norm, row_weight, carried, block_in, first_row):
    length = block_in.shape[0]
    size = block_size(length)

    def inner(position, state):
        moved, column_sums = state
        offset = position * size
        column_rows = lax.dynamic_slice_in_dim(block_in, offset, size, 0)
        bias_part = lax.dynamic_slice_in_dim(bias_row, first_row + offset, size, 0)
        scores = pair_scores(row_proj, column_rows, bias_part)
        backward = (row_weight[:, None] * jnp.exp(scores - row_norm[:, None])).astype(jnp.bfloat16)
        moved = moved + jnp.dot(backward, column_rows, preferred_element_type=jnp.float32)
        column_sums = lax.dynamic_update_slice_in_dim(
            column_sums, jnp.sum(backward.astype(jnp.float32), axis=0), first_row + offset, 0
        )
        return (moved, column_sums)

    return lax.fori_loop(0, length // size, inner, carried)


def shards(particles, log_weight, trans_weight, precision):
    steps_here, rows_here, width = particles.shape
    tm_count = lax.axis_size("tm")
    dom_count = lax.axis_size("dom")
    total_rows = rows_here * dom_count
    tm_place = lax.axis_index("tm")
    is_last = tm_place == tm_count - 1
    weight_full = trans_weight.astype(jnp.float32)
    boundary = from_behind(particles[0], "tm", -1)
    later_sets = [particles[1]] + [boundary]
    later_proj = [project_rows(rows, precision, weight_full) for rows in later_sets]
    biases = []
    for k in range(steps_here):
        predicted = jnp.dot(particles[k], trans_weight.T, preferred_element_type=jnp.float32)
        biases.append(log_weight[k] - 0.5 * jnp.sum(precision * predicted * predicted, axis=1))
    local_bias = jnp.stack(biases)
    full_bias = lax.all_gather(local_bias, "dom", axis=1, tiled=True)
    row_norms = []
    whole = lax.all_gather(particles, "dom", axis=1, tiled=True)
    for k in range(steps_here):
        start_state = (
            jnp.full((rows_here,), -jnp.inf, jnp.float32),
            jnp.zeros((rows_here,), jnp.float32),
        )
        row_top, row_total = make_norm_fold(later_proj[k], full_bias[k], start_state, whole[k], 0)
        row_norms.append(row_top + jnp.log(row_total))
    final_logs = log_weight[steps_here - 1]
    global_top = lax.pmax(jnp.max(final_logs), "dom")
    global_total = lax.psum(jnp.sum(jnp.exp(final_logs - global_top)), "dom")
    final_weights = jnp.exp(final_logs - global_top) / global_total
    carried = (
        jnp.zeros((steps_here, rows_here), jnp.float32),
        jnp.zeros((width, width), jnp.float32),
    )
    for r in range(tm_count):
        if r == 0:
            incoming = jnp.zeros((rows_here,), jnp.float32)
        else:
            incoming = from_behind(carried[0][0], "tm", -1)
        owner = tm_count - 1 - r
        backward_partial_value = jnp.zeros((width, width), jnp.float32)
        outputs = [None] * steps_here
        row_weight = incoming
        for backward_k in range(steps_here - 1, -1, -1):
            column_rows = particles[backward_k]
            backward_start_state = (
                jnp.zeros((rows_here, width), jnp.float32),
                jnp.zeros((total_rows,), jnp.float32),
            )
            moved, column_sums = make_column_fold(
                later_proj[backward_k],
                full_bias[backward_k],
                row_norms[backward_k],
                row_weight,
                backward_start_state,
                whole[backward_k],
                0,
            )
            column_weights = lax.psum_scatter(column_sums, "dom", scatter_dimension=0, tiled=True)
            outer = jnp.dot(
                later_sets[backward_k].astype(jnp.float32).T, moved, precision=exact_mode
            )
            column_float = column_rows.astype(jnp.float32)
            moment = jnp.dot(
                column_float.T * column_weights[None, :], column_float, precision=exact_mode
            )
            backward_partial_value = backward_partial_value + precision[:, None] * (
                outer - jnp.dot(weight_full, moment, precision=exact_mode)
            )
            if backward_k == steps_here - 1:
                column_weights = jnp.where(is_last, final_weights, column_weights)
            outputs[backward_k] = column_weights
            row_weight = column_weights
        is_owner = tm_place == owner
        carried = (
            jnp.where(is_owner, jnp.stack(outputs), carried[0]),
            jnp.where(is_owner, backward_partial_value, carried[1]),
        )
    stacked, partial_value = carried
    score = lax.psum(partial_value, ("dom", "tm"))
    return (stacked * total_rows, score)


def solution(mesh):
    placed = (P("tm", ("seq", "dom"), None), P("tm", ("seq", "dom")), P(), P())
    return jax.shard_map(
        shards,
        mesh=mesh,
        in_specs=placed,
        out_specs=(P("tm", ("seq", "dom")), P("seq", None)),
        check_vma=False,
    )
```

profile of v0, /device:TPU:8, one launch (start us, length us, event | category | flops | bytes accessed | tf_op | source)
XLA Modules:
  0.0 267.3 jit_solution(9784451875654501515)
XLA Ops:
  7.2 0.8 slice_bitcast_fusion.2
  8.0 1.4 collective-permute-start
  9.4 28.6 %all_gather.6 = bf16[2,768,128]{2,1,0:T(8,128)(2,1)S(1)} all-gather(bf16[2,96,128]{2,1,0:T(8,128)(2,1)S(1)} %copy-done.1), channel_id=1, replica_groups=mesh['seq'=2,'dom'=8,'tm'=2] {'dom'}, dimensions={1}, use_global_device_ids=true | all-gather | bytes 442368 | tf_op jit(solution)/shard_map/all_gather | solution.py:93
  38.0 0.3 fusion.54
  38.3 0.3 fusion.53
  38.8 0.6 copy-done.3
  39.4 0.6 slice_reduce_fusion.2
  40.0 22.1 %pmax.7 = f32[]{:T(128)} all-reduce(f32[]{:T(128)} %slice_reduce_fusion.2), channel_id=1, replica_groups=mesh['seq'=2,'dom'=8,'tm'=2] {'dom'}, use_global_device_ids=true, to_apply=%region_3.4 | all-reduce | flops 1 | bytes 8 | tf_op jit(solution)/shard_map/pmax | solution.py:102
  62.1 1.2 fusion.81
  63.3 16.3 %all-gather = f32[8,96,2]{1,2,0:T(2,128)S(1)} all-gather(f32[1,96,2]{1,2,0:T(2,128)S(1)} %maximum_bitcast_fusion), channel_id=1, replica_groups=mesh['seq'=2,'dom'=8,'tm'=2] {'dom'}, dimensions={0}, use_global_device_ids=true | all-gather | bytes 6912 | tf_op jit(solution)/shard_map/all_gather | solution.py:91
  79.7 1.2 while.98
  79.8 0.3 fusion.143
  80.4 0.3 fusion.143
  81.0 0.6 copy-done.4
  81.7 0.6 dynamic-slice
  83.1 1.2 while.96
  83.2 0.3 fusion.136
  83.7 0.3 fusion.136
  84.3 1.5 while.97
  84.8 0.2 dynamic_update_slice.36
  85.5 0.2 dynamic_update_slice.36
  85.8 19.9 %all-reduce.4 = (f32[768]{0:T(1024)S(1)}, f32[]{:T(128)}) all-reduce(f32[768]{0:T(1024)S(1)} %get-tuple-element.769, f32[]{:T(128)} %get-tuple-element.1041), channel_id=2, replica_groups=mesh['seq'=2,'dom'=8,'tm'=2] {'dom'}, use_global_device_ids=true, to_apply=%region_13.0.clone | all-reduce | flops 769 | bytes 6152
  105.6 1.3 broadcast_select_fusion.5
  106.9 1.5 while.99
  107.4 0.2 dynamic_update_slice.37
  108.1 0.2 dynamic_update_slice.37
  108.4 17.1 %all-reduce.1 = f32[768]{0:T(1024)S(1)} all-reduce(f32[768]{0:T(1024)S(1)} %get-tuple-element.772), channel_id=3, replica_groups=mesh['seq'=2,'dom'=8,'tm'=2] {'dom'}, use_global_device_ids=true, to_apply=%region_21.22.clone | all-reduce | flops 768 | bytes 6144
  125.6 1.3 collective-permute-start.1
  127.2 0.3 fusion.52
  127.5 0.3 fusion.50
  127.8 0.2 fusion.86
  128.1 0.2 convolution_subtract_fusion
  128.3 0.3 fusion.44
  128.7 1.5 while.100
  129.1 0.2 dynamic_update_slice.38
  129.9 0.2 dynamic_update_slice.38
  130.1 19.1 %all-reduce.2 = f32[768]{0:T(1024)S(1)} all-reduce(f32[768]{0:T(1024)S(1)} %get-tuple-element.773), channel_id=4, replica_groups=mesh['seq'=2,'dom'=8,'tm'=2] {'dom'}, use_global_device_ids=true, to_apply=%region_25.26.clone | all-reduce | flops 768 | bytes 6144
  149.3 1.5 while.101
  149.8 0.2 dynamic_update_slice.39
  150.5 0.2 dynamic_update_slice.39
  150.8 17.1 %all-reduce.3 = f32[768]{0:T(1024)S(1)} all-reduce(f32[768]{0:T(1024)S(1)} %get-tuple-element.774), channel_id=5, replica_groups=mesh['seq'=2,'dom'=8,'tm'=2] {'dom'}, use_global_device_ids=true, to_apply=%region_29.30.clone | all-reduce | flops 768 | bytes 6144
  168.3 0.3 fusion.51
  168.6 0.3 fusion.49
  169.2 0.2 convolution_subtract_fusion.2
  169.4 0.9 fusion.48
  170.4 0.6 fusion.80
  170.9 88.0 %all-reduce.7.cloned.1.call-done = f32[128,128]{0,1:T(8,128)} async-done(((f32[128,128]{0,1:T(8,128)}), f32[128,128]{0,1:T(8,128)}) %all-reduce.7.cloned.1.call-update) | async-done | bytes 65552 | tf_op jit(solution)/shard_map/psum | solution.py:154
  258.9 1.6 copy.10
  (86 shorter events, 6.6 us)
Async XLA Ops:
  7.2 30.9 %copy-start = (bf16[128,128]{1,0:T(8,128)(2,1)S(1)}, bf16[128,128]{1,0:T(8,128)(2,1)}, u32[]{:S(2)}) copy-start(bf16[128,128]{1,0:T(8,128)(2,1)} %param.18) | copy-start | bytes 98308
  7.2 2.2 copy-start.1
  7.2 251.7 %all-reduce.7.cloned.1.call-start = ((), (), s32[]{:S(2)}) async-start(), calls=%async_computation | async-start | bytes 131072 | tf_op jit(solution)/shard_map/psum | solution.py:154
  8.0 30.0 %copy-start.2 = (f32[128]{0:T(128)S(1)}, f32[128]{0:T(128)}, u32[]{:S(2)}) copy-start(f32[128]{0:T(128)} %param.19) | copy-start | bytes 1540
  8.0 74.9 %collective-permute-start = (bf16[96,128]{1,0:T(8,128)(2,1)S(1)}, bf16[96,128]{1,0:T(8,128)(2,1)S(1)}, u32[]{:S(2)}, u32[]{:S(2)}) collective-permute-start(bf16[96,128]{1,0:T(8,128)(2,1)S(1)} %slice_bitcast_fusion.2), channel_id=1, source_target_pairs={{1,0},{3,2},{5,4},{7,6},{9,8},{11,10},{13,12},{15,14},{17,16},{19,... | collective-permute-start | bytes 73736 | tf_op jit(solution)/shard_map/ppermute | solution.py:12
  38.7 0.7 copy-start.3
  81.0 0.7 copy-start.4
  125.6 3.0 %collective-permute-start.1 = (f32[96]{0:T(128)S(1)}, f32[96]{0:T(128)S(1)}, u32[]{:S(2)}, u32[]{:S(2)}) collective-permute-start(f32[96]{0:T(128)S(1)} %slice_bitcast_fusion.3), channel_id=1, source_target_pairs={{1,0},{3,2},{5,4},{7,6},{9,8},{11,10},{13,12},{15,14},{17,16},{19,... | collective-permute-start | bytes 1160 | tf_op jit(solution)/shard_map/ppermute | solution.py:12
Sparse Core Ops, SparseCore 0:
  170.5 88.4 all-reduce.6
where the time goes:
time: 268 us; the launch traced here: 267 us
  blocking collectives  140 us (52%)
  waiting for transfers between devices  88.1 us (33%)
  between operations  14.9 us (6%)
  matrix products  8.92 us (3%)
  local copies, waits for them, and re-layouts  7.58 us (3%)
  other arithmetic  4.58 us (2%)
  starting transfers between devices  2.74 us (1%)
    psum x1, waiting for transfers between devices, shards(): score = lax.psum(partial_value, ('dom', 'tm'))  88 us
    unnamed x4, blocking collectives  73.2 us
    all_gather x1, blocking collectives, shards(): whole = lax.all_gather(particles, 'dom', axis=1, tiled=True)  28.6 us
    pmax x1, blocking collectives, shards(): global_top = lax.pmax(jnp.max(final_logs), 'dom')  22.1 us
    all_gather x1, blocking collectives, shards(): full_bias = lax.all_gather(local_bias, 'dom', axis=1, tiled=True)  16.3 us
  transfers between devices with their start and end apart: 3, of which 2 were waited for; matrix products, arithmetic and copies ran while one was open for 2% of the time, Pallas kernels for 0%

commit v1 on v0

--- a/solution.py
+++ b/solution.py
@@ -151,7 +151,7 @@
             jnp.where(is_owner, backward_partial_value, carried[1]),
         )
     stacked, partial_value = carried
-    score = lax.psum(partial_value, ("dom", "tm"))
+    score = lax.psum(lax.psum(partial_value, "tm"), "dom")
     return (stacked * total_rows, score)
 
 

time: 268 us -> 273 us (1.019)
  waiting for transfers between devices: 88.1 us -> 92 us
    psum x1 -> x2, waiting for transfers between devices: 88 us -> 91.9 us  [shards(): score = lax.psum(lax.psum(partial_value, 'tm'), 'dom')]
  transfers between devices with their start and end apart: 3 -> 4, of which waited for: 2 -> 3; matrix products, arithmetic and copies ran while one was open for 2% -> 2% of each run, Pallas kernels for 0% -> 0%
where the time goes in v1:
time: 273 us; the launch traced here: 271 us
  blocking collectives  140 us (51%)
  waiting for transfers between devices  92 us (34%)
  between operations  14.9 us (5%)
  matrix products  8.93 us (3%)
  local copies, waits for them, and re-layouts  7.58 us (3%)
  other arithmetic  4.58 us (2%)
  starting transfers between devices  2.78 us (1%)
    psum x2, waiting for transfers between devices, shards(): score = lax.psum(lax.psum(partial_value, 'tm'), 'dom')  91.9 us
    unnamed x4, blocking collectives  73.2 us
    all_gather x1, blocking collectives, shards(): whole = lax.all_gather(particles, 'dom', axis=1, tiled=True)  28.6 us
    pmax x1, blocking collectives, shards(): global_top = lax.pmax(jnp.max(final_logs), 'dom')  22.1 us
    all_gather x1, blocking collectives, shards(): full_bias = lax.all_gather(local_bias, 'dom', axis=1, tiled=True)  16.3 us
  transfers between devices with their start and end apart: 4, of which 3 were waited for; matrix products, arithmetic and copies ran while one was open for 2% of the time, Pallas kernels for 0%

profile of v1, /device:TPU:8, one launch (start us, length us, event | category | flops | bytes accessed | tf_op | source)
XLA Modules:
  0.0 271.3 jit_solution(8518882286427378207)
XLA Ops:
  7.2 0.8 slice_bitcast_fusion.2
  8.0 1.4 collective-permute-start
  9.4 28.6 %all_gather.6 = bf16[2,768,128]{2,1,0:T(8,128)(2,1)S(1)} all-gather(bf16[2,96,128]{2,1,0:T(8,128)(2,1)S(1)} %copy-done.1), channel_id=1, replica_groups=mesh['seq'=2,'dom'=8,'tm'=2] {'dom'}, dimensions={1}, use_global_device_ids=true | all-gather | bytes 442368 | tf_op jit(solution)/shard_map/all_gather | solution.py:93
  38.0 0.3 fusion.54
  38.3 0.3 fusion.53
  38.8 0.6 copy-done.3
  39.4 0.6 slice_reduce_fusion.2
  40.0 22.1 %pmax.7 = f32[]{:T(128)} all-reduce(f32[]{:T(128)} %slice_reduce_fusion.2), channel_id=1, replica_groups=mesh['seq'=2,'dom'=8,'tm'=2] {'dom'}, use_global_device_ids=true, to_apply=%region_3.4 | all-reduce | flops 1 | bytes 8 | tf_op jit(solution)/shard_map/pmax | solution.py:102
  62.1 1.2 fusion.81
  63.3 16.3 %all-gather = f32[8,96,2]{1,2,0:T(2,128)S(1)} all-gather(f32[1,96,2]{1,2,0:T(2,128)S(1)} %maximum_bitcast_fusion), channel_id=1, replica_groups=mesh['seq'=2,'dom'=8,'tm'=2] {'dom'}, dimensions={0}, use_global_device_ids=true | all-gather | bytes 6912 | tf_op jit(solution)/shard_map/all_gather | solution.py:91
  79.7 1.2 while.98
  79.8 0.3 fusion.143
  80.4 0.3 fusion.143
  81.0 0.6 copy-done.4
  81.7 0.6 dynamic-slice
  83.1 1.2 while.96
  83.2 0.3 fusion.136
  83.7 0.3 fusion.136
  84.3 1.5 while.97
  84.8 0.2 dynamic_update_slice.36
  85.5 0.2 dynamic_update_slice.36
  85.8 19.9 %all-reduce.4 = (f32[768]{0:T(1024)S(1)}, f32[]{:T(128)}) all-reduce(f32[768]{0:T(1024)S(1)} %get-tuple-element.769, f32[]{:T(128)} %get-tuple-element.1041), channel_id=2, replica_groups=mesh['seq'=2,'dom'=8,'tm'=2] {'dom'}, use_global_device_ids=true, to_apply=%region_13.0.clone | all-reduce | flops 769 | bytes 6152
  105.6 1.3 broadcast_select_fusion.5
  106.9 1.5 while.99
  107.4 0.2 dynamic_update_slice.37
  108.1 0.2 dynamic_update_slice.37
  108.4 17.1 %all-reduce.1 = f32[768]{0:T(1024)S(1)} all-reduce(f32[768]{0:T(1024)S(1)} %get-tuple-element.772), channel_id=3, replica_groups=mesh['seq'=2,'dom'=8,'tm'=2] {'dom'}, use_global_device_ids=true, to_apply=%region_21.22.clone | all-reduce | flops 768 | bytes 6144
  125.6 1.3 collective-permute-start.1
  127.2 0.3 fusion.52
  127.5 0.3 fusion.50
  128.1 0.2 convolution_subtract_fusion
  128.3 0.3 fusion.44
  128.7 1.5 while.100
  129.1 0.2 dynamic_update_slice.38
  129.9 0.2 dynamic_update_slice.38
  130.1 19.1 %all-reduce.2 = f32[768]{0:T(1024)S(1)} all-reduce(f32[768]{0:T(1024)S(1)} %get-tuple-element.773), channel_id=4, replica_groups=mesh['seq'=2,'dom'=8,'tm'=2] {'dom'}, use_global_device_ids=true, to_apply=%region_25.26.clone | all-reduce | flops 768 | bytes 6144
  149.3 1.5 while.101
  149.8 0.2 dynamic_update_slice.39
  150.5 0.2 dynamic_update_slice.39
  150.8 17.1 %all-reduce.3 = f32[768]{0:T(1024)S(1)} all-reduce(f32[768]{0:T(1024)S(1)} %get-tuple-element.774), channel_id=5, replica_groups=mesh['seq'=2,'dom'=8,'tm'=2] {'dom'}, use_global_device_ids=true, to_apply=%region_29.30.clone | all-reduce | flops 768 | bytes 6144
  168.2 0.3 fusion.51
  168.5 0.3 fusion.49
  169.1 0.2 convolution_subtract_fusion.2
  169.4 0.9 fusion.48
  170.4 19.5 %all-reduce.8.cloned.1.call-done = f32[128,128]{0,1:T(8,128)} async-done(((f32[128,128]{0,1:T(8,128)}), f32[128,128]{0,1:T(8,128)}) %all-reduce.8.cloned.1.call-update) | async-done | bytes 65552 | tf_op jit(solution)/shard_map/psum | solution.py:154
  189.9 0.6 fusion.80
  190.5 72.4 %all-reduce.10.cloned.1.call-done = f32[128,128]{0,1:T(8,128)} async-done(((f32[128,128]{0,1:T(8,128)}), f32[128,128]{0,1:T(8,128)}) %all-reduce.10.cloned.1.call-update) | async-done | bytes 65552 | tf_op jit(solution)/shard_map/psum | solution.py:154
  262.9 1.6 copy.10
  (89 shorter events, 6.9 us)
Async XLA Ops:
  7.2 30.9 %copy-start = (bf16[128,128]{1,0:T(8,128)(2,1)S(1)}, bf16[128,128]{1,0:T(8,128)(2,1)}, u32[]{:S(2)}) copy-start(bf16[128,128]{1,0:T(8,128)(2,1)} %param.18) | copy-start | bytes 98308
  7.2 2.2 copy-start.1
  7.2 182.7 %all-reduce.8.cloned.1.call-start = ((), (), s32[]{:S(2)}) async-start(), calls=%async_computation | async-start | bytes 131072 | tf_op jit(solution)/shard_map/psum | solution.py:154
  8.0 30.0 %copy-start.2 = (f32[128]{0:T(128)S(1)}, f32[128]{0:T(128)}, u32[]{:S(2)}) copy-start(f32[128]{0:T(128)} %param.19) | copy-start | bytes 1540
  8.0 74.9 %collective-permute-start = (bf16[96,128]{1,0:T(8,128)(2,1)S(1)}, bf16[96,128]{1,0:T(8,128)(2,1)S(1)}, u32[]{:S(2)}, u32[]{:S(2)}) collective-permute-start(bf16[96,128]{1,0:T(8,128)(2,1)S(1)} %slice_bitcast_fusion.2), channel_id=1, source_target_pairs={{1,0},{3,2},{5,4},{7,6},{9,8},{11,10},{13,12},{15,14},{17,16},{19,... | collective-permute-start | bytes 73736 | tf_op jit(solution)/shard_map/ppermute | solution.py:12
  38.7 0.7 copy-start.3
  81.0 0.7 copy-start.4
  125.6 3.0 %collective-permute-start.1 = (f32[96]{0:T(128)S(1)}, f32[96]{0:T(128)S(1)}, u32[]{:S(2)}, u32[]{:S(2)}) collective-permute-start(f32[96]{0:T(128)S(1)} %slice_bitcast_fusion.3), channel_id=1, source_target_pairs={{1,0},{3,2},{5,4},{7,6},{9,8},{11,10},{13,12},{15,14},{17,16},{19,... | collective-permute-start | bytes 1160 | tf_op jit(solution)/shard_map/ppermute | solution.py:12
  170.3 92.6 %all-reduce.10.cloned.1.call-start = ((), (), s32[]{:S(2)}) async-start(), calls=%async_computation.1 | async-start | bytes 131072 | tf_op jit(solution)/shard_map/psum | solution.py:154
Sparse Core Ops, SparseCore 0:
  170.4 19.4 all-reduce.7
  193.3 69.5 all-reduce.9
